TPU v7x, 32 devices: a whole 2x2x4 slice. The times are simulated.
32 devices in a mesh: grp: 2 (over x), had: 16 (over z, y, core).
Axes of the slice: x: 2, y: 2, z: 4, core: 2. Of those that a mesh axis runs over, the one named last changes fastest.
Arguments:
- source_slabs: bfloat16 [512, 128, 128], P(('grp', 'had')), parts along dimension 0, may hold values from -6 to 6
- sink_slabs: bfloat16 [512, 128, 128], P(('grp', 'had')), parts along dimension 0, may hold values from -6 to 6
- perambulators: bfloat16 [4, 2, 128, 128], P('grp'), parts along dimension 0, may hold values from -0.5 to 0.5
- send_pick: int32 [32, 16], P(('grp', 'had')), parts along dimension 0, may hold values from 0 to 15
- graph_slot: int32 [32, 512, 2], P(('grp', 'had')), parts along dimension 0, may hold values from 0 to 15
- graph_sink: int32 [32, 512, 2], P(('grp', 'had')), parts along dimension 0, may hold values from 0 to 15
- graph_count: int32 [32], P(('grp', 'had')), parts along dimension 0, may hold values from 64 to 512, as said below
- pair_list: int32 [256, 2], P(('grp', 'had')), parts along dimension 0, may hold values from 0 to 15
Outputs:
- edge_matrices: bfloat16 [32, 128, 128], P(('grp', 'had')), parts along dimension 0
- pair_products: bfloat16 [256, 128, 128], P(('grp', 'had')), parts along dimension 0
There are 2 independent parts, one for each index of `grp`. A program takes and returns all parts, laid end to end along the dimension named above; each array names one. Nothing has to cross between parts.
Inputs may be any that keep to these rules, and one draw needn't show every extreme that they name: Some reader uses all 512 graph slots; slots from graph_count on are unused.
All inputs are finite; a program needn't handle non-finite values.
Results may differ from a plain program's by a relative error of at most 0.012.
Values may be sent and summed in bfloat16 or wider, within the bound.
A program may use at most 64 MiB of HBM per device.

v0:
```python
import math
import jax
import jax.numpy as jnp
from jax import lax
from jax.sharding import PartitionSpec as P


def shards(
    source_slabs,
    sink_slabs,
    perambulators,
    send_pick,
    graph_slot,
    graph_sink,
    graph_count,
    pair_list,
):
    my_index = lax.axis_index("had")
    evecs = source_slabs.shape[1]
    per_device = source_slabs.shape[0]
    root_scale = 1.0 / math.sqrt(evecs)
    edge_scale = 1.0 / math.sqrt(evecs * graph_slot.shape[1])
    timeslice = my_index * per_device // evecs
    local_peram = lax.dynamic_index_in_dim(perambulators, timeslice, 0, keepdims=False)
    first_turn = jnp.einsum(
        "xa,jab->xjb", local_peram[0], source_slabs, preferred_element_type=jnp.float32
    ).astype(jnp.bfloat16)
    pick_row = send_pick[0]
    second_turn = jnp.einsum(
        "xjb,yb->xjy", first_turn, local_peram[1], preferred_element_type=jnp.float32
    ).astype(jnp.bfloat16)
    outgoing = jnp.take(second_turn, pick_row, axis=1)
    received = lax.all_to_all(outgoing, "had", split_axis=1, concat_axis=1, tiled=True)
    graph_rows = graph_slot.shape[1]
    block_width = min(64, graph_rows)
    slot_table = graph_slot[0]
    sink_table = graph_sink[0]
    graph_total = graph_count[0]

    def factor(slots, sinks):
        gathered = jnp.take(received, slots, axis=1)
        resident = jnp.take(sink_slabs, sinks, axis=0)
        product = jnp.einsum("gxb,agb->gxa", resident, gathered, preferred_element_type=jnp.float32)
        return (product * root_scale).astype(jnp.bfloat16)

    def accumulate(block_index, running_sum):
        offset = block_index * block_width
        slots = lax.dynamic_slice_in_dim(slot_table, offset, block_width, 0)
        sinks = lax.dynamic_slice_in_dim(sink_table, offset, block_width, 0)
        is_valid = (offset + jnp.arange(block_width, dtype=jnp.int32) < graph_total).astype(
            jnp.bfloat16
        )
        left_side = factor(slots[:, 0], sinks[:, 0]) * is_valid[:, None, None]
        right_side = factor(slots[:, 1], sinks[:, 1])
        return running_sum + jnp.einsum(
            "gxa,gay->xy", left_side, right_side, preferred_element_type=jnp.float32
        )

    block_count = (graph_total + block_width - 1) // block_width
    summed = lax.fori_loop(0, block_count, accumulate, jnp.zeros((evecs, evecs), jnp.float32))
    edge_local = (summed * edge_scale).astype(jnp.bfloat16)[None]
    left_ids = pair_list[:, 0]
    right_ids = pair_list[:, 1]
    shard_rows = lax.all_gather(edge_local, "had", axis=0, tiled=True)
    row_ids = jnp.arange(shard_rows.shape[0], dtype=jnp.int32)
    left_select = (left_ids[:, None] == row_ids[None, :]).astype(jnp.bfloat16)
    right_select = (right_ids[:, None] == row_ids[None, :]).astype(jnp.bfloat16)
    left_part = jnp.einsum(
        "pn,nxy->pxy", left_select, shard_rows, preferred_element_type=jnp.float32
    )
    right_part = jnp.einsum(
        "pn,nxy->pxy", right_select, shard_rows, preferred_element_type=jnp.float32
    )
    left_edges = left_part.astype(jnp.bfloat16)
    right_edges = right_part.astype(jnp.bfloat16)
    product = jnp.einsum(
        "pxa,pay->pxy", left_edges, right_edges, preferred_element_type=jnp.float32
    )
    pair_products = (product * root_scale).astype(jnp.bfloat16)
    return (edge_local, pair_products)


def solution(mesh):
    return jax.shard_map(
        shards,
        mesh=mesh,
        in_specs=(
            P(("grp", "had"), None, None),
            P(("grp", "had"), None, None),
            P("grp", None, None, None),
            P(("grp", "had"), None),
            P(("grp", "had"), None, None),
            P(("grp", "had"), None, None),
            P(("grp", "had")),
            P(("grp", "had"), None),
        ),
        out_specs=(P(("grp", "had"), None, None), P(("grp", "had"), None, None)),
        check_vma=False,
    )
```

profile of v0, /device:TPU:0, one launch (start us, length us, event | category | flops | bytes accessed | tf_op | source)
XLA Modules:
  0.0 210.6 jit_solution(10187311681063074676)
XLA Ops:
  0.6 0.0 copy-start
  0.7 0.7 fusion.45
  1.4 0.7 compare_and_fusion.4
  2.0 0.0 copy-done
  2.1 0.0 copy-start.2
  2.1 0.0 copy-start.1
  2.1 1.3 convolution_convert_fusion
  3.4 0.6 gather_fusion.4
  4.1 0.9 select_bitcast_fusion
  5.0 7.4 %all-to-all-start = ((bf16[128,16,128]{2,0,1:T(8,128)(2,1)}), bf16[128,16,128]{2,0,1:T(8,128)(2,1)S(1)}, u32[]{:S(2)}, u32[]{:S(2)}) async-start(bf16[128,16,128]{2,0,1:T(8,128)(2,1)} %select_bitcast_fusion), calls=%async_computation | async-start | bytes 1048576 | tf_op jit(solution)/shard_map/all_to_all | solution.py:33
  13.1 0.0 copy-done.2
  13.1 13.6 %all-to-all-done = bf16[128,16,128]{2,0,1:T(8,128)(2,1)S(1)} async-done(((bf16[128,16,128]{2,0,1:T(8,128)(2,1)}), bf16[128,16,128]{2,0,1:T(8,128)(2,1)S(1)}, u32[]{:S(2)}, u32[]{:S(2)}) %all-to-all-start) | async-done | bytes 524320 | tf_op jit(solution)/shard_map/all_to_all | solution.py:33
  26.7 0.0 copy-done.1
  26.7 81.4 %while.10 = (s32[]{:T(128)}, f32[128,128]{1,0:T(8,128)S(1)}, s32[]{:T(128)}, s32[512,2]{0,1:T(2,128)}, bf16[16,128,128]{2,1,0:T(8,128)(2,1)S(1)}, /*index=5*/s32...) while((s32[]{:T(128)}, f32[128,128]{1,0:T(8,128)S(1)}, ...), condition=%wide.region_1.4_spmd, body=%wide.region_0.3_spmd.sunk | while | flops 814765760 | bytes 29514672 | solution.py:60
  26.7 0.8 constant_dynamic-slice_fusion.3
  27.5 2.1 %gather_fusion = bf16[64,128,128]{2,1,0:T(8,128)(2,1)} fusion(bf16[128,16,128]{2,0,1:T(8,128)(2,1)S(1)} %get-tuple-element.188, s32[1024]{0:T(1024)S(1)} %pad_clamp_fusion.9), kind=kCustom, calls=%fused_computation.3.clone.clone.1 | custom fusion | bytes 4194560 | tf_op jit(solution)/shard_map/while/body/jit(_take)/gather | solution.py:41
  29.7 2.1 %gather_fusion.1 = bf16[64,128,128]{2,1,0:T(8,128)(2,1)} fusion(bf16[16,128,128]{2,1,0:T(8,128)(2,1)S(1)} %get-tuple-element.186, s32[1024]{0:T(1024)S(1)} %pad_clamp_fusion.10), kind=kCustom, calls=%fused_computation.2.clone.clone.1 | custom fusion | bytes 4194560 | tf_op jit(solution)/shard_map/while/body/jit(_take)/gather | solution.py:42
  31.8 5.2 %multiply_convert_fusion.4 = bf16[64,128,128]{2,1,0:T(8,128)(2,1)} fusion(bf16[64,128,128]{2,1,0:T(8,128)(2,1)} %gather_fusion, bf16[64,128,128]{2,1,0:T(8,128)(2,1)} %gather_fusion.1, pred[64]{0:T(512)(128)(4,1)S(1)} %get-tuple-element.152, pred[64]{0:T(512)(128)(4,1)S(1)} %get-tuple-element.153), kind=kOutput, calls=%fused_computation.5.clone.1 | convolution fusion | flops 272629760 | bytes 6291584 | tf_op jit(solution)/shard_map/while/body/gxb,agb->gxa/dot_general | solution.py:43
  37.0 2.1 %gather_fusion.2 = bf16[64,128,128]{2,1,0:T(8,128)(2,1)} fusion(bf16[128,16,128]{2,0,1:T(8,128)(2,1)S(1)} %get-tuple-element.188, s32[1024]{0:T(1024)S(1)} %pad_clamp_fusion.11), kind=kCustom, calls=%fused_computation.1.clone.clone.1 | custom fusion | bytes 4194560 | tf_op jit(solution)/shard_map/while/body/jit(_take)/gather | solution.py:41
  39.1 2.1 %gather_fusion.3 = bf16[64,128,128]{2,1,0:T(8,128)(2,1)} fusion(bf16[16,128,128]{2,1,0:T(8,128)(2,1)S(1)} %get-tuple-element.186, s32[1024]{0:T(1024)S(1)} %pad_clamp_fusion.12), kind=kCustom, calls=%fused_computation.clone.clone.1 | custom fusion | bytes 4194560 | tf_op jit(solution)/shard_map/while/body/jit(_take)/gather | solution.py:42
  41.3 0.6 compare_convert_fusion.2
  41.9 5.1 %fusion.64 = f32[128,128]{1,0:T(8,128)S(1)} fusion(f32[128,128]{1,0:T(8,128)S(1)} %get-tuple-element.171, bf16[64,128,128]{2,1,0:T(8,128)(2,1)} %multiply_convert_fusion.4, bf16[64,128,128]{2,1,0:T(8,128)(2,1)} %gather_fusion.2, bf16[64,128,128]{2,1,0:T(8,128)(2,1)} %gather_fusion.3, pred[64]{0:T(512)(128)(4,1)S(1)} %get-tuple-element.156, ...), kind=kOutput, calls=%fused_computation.20.clone.1 | convolution fusion | flops 542130176 | bytes 6422784 | tf_op jit(solution)/shard_map/while/body/gxa,gay->xy/dot_general | solution.py:55
  47.1 0.8 constant_dynamic-slice_fusion.3
  47.9 2.1 %gather_fusion = bf16[64,128,128]{2,1,0:T(8,128)(2,1)} fusion(bf16[128,16,128]{2,0,1:T(8,128)(2,1)S(1)} %get-tuple-element.188, s32[1024]{0:T(1024)S(1)} %pad_clamp_fusion.9), kind=kCustom, calls=%fused_computation.3.clone.clone.1 | custom fusion | bytes 4194560 | tf_op jit(solution)/shard_map/while/body/jit(_take)/gather | solution.py:41
  50.0 2.1 %gather_fusion.1 = bf16[64,128,128]{2,1,0:T(8,128)(2,1)} fusion(bf16[16,128,128]{2,1,0:T(8,128)(2,1)S(1)} %get-tuple-element.186, s32[1024]{0:T(1024)S(1)} %pad_clamp_fusion.10), kind=kCustom, calls=%fused_computation.2.clone.clone.1 | custom fusion | bytes 4194560 | tf_op jit(solution)/shard_map/while/body/jit(_take)/gather | solution.py:42
  52.1 5.2 %multiply_convert_fusion.4 = bf16[64,128,128]{2,1,0:T(8,128)(2,1)} fusion(bf16[64,128,128]{2,1,0:T(8,128)(2,1)} %gather_fusion, bf16[64,128,128]{2,1,0:T(8,128)(2,1)} %gather_fusion.1, pred[64]{0:T(512)(128)(4,1)S(1)} %get-tuple-element.152, pred[64]{0:T(512)(128)(4,1)S(1)} %get-tuple-element.153), kind=kOutput, calls=%fused_computation.5.clone.1 | convolution fusion | flops 272629760 | bytes 6291584 | tf_op jit(solution)/shard_map/while/body/gxb,agb->gxa/dot_general | solution.py:43
  57.4 2.1 %gather_fusion.2 = bf16[64,128,128]{2,1,0:T(8,128)(2,1)} fusion(bf16[128,16,128]{2,0,1:T(8,128)(2,1)S(1)} %get-tuple-element.188, s32[1024]{0:T(1024)S(1)} %pad_clamp_fusion.11), kind=kCustom, calls=%fused_computation.1.clone.clone.1 | custom fusion | bytes 4194560 | tf_op jit(solution)/shard_map/while/body/jit(_take)/gather | solution.py:41
  59.5 2.1 %gather_fusion.3 = bf16[64,128,128]{2,1,0:T(8,128)(2,1)} fusion(bf16[16,128,128]{2,1,0:T(8,128)(2,1)S(1)} %get-tuple-element.186, s32[1024]{0:T(1024)S(1)} %pad_clamp_fusion.12), kind=kCustom, calls=%fused_computation.clone.clone.1 | custom fusion | bytes 4194560 | tf_op jit(solution)/shard_map/while/body/jit(_take)/gather | solution.py:42
  61.6 0.6 compare_convert_fusion.2
  62.3 5.1 %fusion.64 = f32[128,128]{1,0:T(8,128)S(1)} fusion(f32[128,128]{1,0:T(8,128)S(1)} %get-tuple-element.171, bf16[64,128,128]{2,1,0:T(8,128)(2,1)} %multiply_convert_fusion.4, bf16[64,128,128]{2,1,0:T(8,128)(2,1)} %gather_fusion.2, bf16[64,128,128]{2,1,0:T(8,128)(2,1)} %gather_fusion.3, pred[64]{0:T(512)(128)(4,1)S(1)} %get-tuple-element.156, ...), kind=kOutput, calls=%fused_computation.20.clone.1 | convolution fusion | flops 542130176 | bytes 6422784 | tf_op jit(solution)/shard_map/while/body/gxa,gay->xy/dot_general | solution.py:55
  67.4 0.8 constant_dynamic-slice_fusion.3
  68.2 2.1 %gather_fusion = bf16[64,128,128]{2,1,0:T(8,128)(2,1)} fusion(bf16[128,16,128]{2,0,1:T(8,128)(2,1)S(1)} %get-tuple-element.188, s32[1024]{0:T(1024)S(1)} %pad_clamp_fusion.9), kind=kCustom, calls=%fused_computation.3.clone.clone.1 | custom fusion | bytes 4194560 | tf_op jit(solution)/shard_map/while/body/jit(_take)/gather | solution.py:41
  70.4 2.1 %gather_fusion.1 = bf16[64,128,128]{2,1,0:T(8,128)(2,1)} fusion(bf16[16,128,128]{2,1,0:T(8,128)(2,1)S(1)} %get-tuple-element.186, s32[1024]{0:T(1024)S(1)} %pad_clamp_fusion.10), kind=kCustom, calls=%fused_computation.2.clone.clone.1 | custom fusion | bytes 4194560 | tf_op jit(solution)/shard_map/while/body/jit(_take)/gather | solution.py:42
  72.5 5.2 %multiply_convert_fusion.4 = bf16[64,128,128]{2,1,0:T(8,128)(2,1)} fusion(bf16[64,128,128]{2,1,0:T(8,128)(2,1)} %gather_fusion, bf16[64,128,128]{2,1,0:T(8,128)(2,1)} %gather_fusion.1, pred[64]{0:T(512)(128)(4,1)S(1)} %get-tuple-element.152, pred[64]{0:T(512)(128)(4,1)S(1)} %get-tuple-element.153), kind=kOutput, calls=%fused_computation.5.clone.1 | convolution fusion | flops 272629760 | bytes 6291584 | tf_op jit(solution)/shard_map/while/body/gxb,agb->gxa/dot_general | solution.py:43
  77.7 2.1 %gather_fusion.2 = bf16[64,128,128]{2,1,0:T(8,128)(2,1)} fusion(bf16[128,16,128]{2,0,1:T(8,128)(2,1)S(1)} %get-tuple-element.188, s32[1024]{0:T(1024)S(1)} %pad_clamp_fusion.11), kind=kCustom, calls=%fused_computation.1.clone.clone.1 | custom fusion | bytes 4194560 | tf_op jit(solution)/shard_map/while/body/jit(_take)/gather | solution.py:41
  79.8 2.1 %gather_fusion.3 = bf16[64,128,128]{2,1,0:T(8,128)(2,1)} fusion(bf16[16,128,128]{2,1,0:T(8,128)(2,1)S(1)} %get-tuple-element.186, s32[1024]{0:T(1024)S(1)} %pad_clamp_fusion.12), kind=kCustom, calls=%fused_computation.clone.clone.1 | custom fusion | bytes 4194560 | tf_op jit(solution)/shard_map/while/body/jit(_take)/gather | solution.py:42
  82.0 0.6 compare_convert_fusion.2
  82.6 5.1 %fusion.64 = f32[128,128]{1,0:T(8,128)S(1)} fusion(f32[128,128]{1,0:T(8,128)S(1)} %get-tuple-element.171, bf16[64,128,128]{2,1,0:T(8,128)(2,1)} %multiply_convert_fusion.4, bf16[64,128,128]{2,1,0:T(8,128)(2,1)} %gather_fusion.2, bf16[64,128,128]{2,1,0:T(8,128)(2,1)} %gather_fusion.3, pred[64]{0:T(512)(128)(4,1)S(1)} %get-tuple-element.156, ...), kind=kOutput, calls=%fused_computation.20.clone.1 | convolution fusion | flops 542130176 | bytes 6422784 | tf_op jit(solution)/shard_map/while/body/gxa,gay->xy/dot_general | solution.py:55
  87.8 0.8 constant_dynamic-slice_fusion.3
  88.6 2.1 %gather_fusion = bf16[64,128,128]{2,1,0:T(8,128)(2,1)} fusion(bf16[128,16,128]{2,0,1:T(8,128)(2,1)S(1)} %get-tuple-element.188, s32[1024]{0:T(1024)S(1)} %pad_clamp_fusion.9), kind=kCustom, calls=%fused_computation.3.clone.clone.1 | custom fusion | bytes 4194560 | tf_op jit(solution)/shard_map/while/body/jit(_take)/gather | solution.py:41
  90.7 2.1 %gather_fusion.1 = bf16[64,128,128]{2,1,0:T(8,128)(2,1)} fusion(bf16[16,128,128]{2,1,0:T(8,128)(2,1)S(1)} %get-tuple-element.186, s32[1024]{0:T(1024)S(1)} %pad_clamp_fusion.10), kind=kCustom, calls=%fused_computation.2.clone.clone.1 | custom fusion | bytes 4194560 | tf_op jit(solution)/shard_map/while/body/jit(_take)/gather | solution.py:42
  92.8 5.2 %multiply_convert_fusion.4 = bf16[64,128,128]{2,1,0:T(8,128)(2,1)} fusion(bf16[64,128,128]{2,1,0:T(8,128)(2,1)} %gather_fusion, bf16[64,128,128]{2,1,0:T(8,128)(2,1)} %gather_fusion.1, pred[64]{0:T(512)(128)(4,1)S(1)} %get-tuple-element.152, pred[64]{0:T(512)(128)(4,1)S(1)} %get-tuple-element.153), kind=kOutput, calls=%fused_computation.5.clone.1 | convolution fusion | flops 272629760 | bytes 6291584 | tf_op jit(solution)/shard_map/while/body/gxb,agb->gxa/dot_general | solution.py:43
  98.1 2.1 %gather_fusion.2 = bf16[64,128,128]{2,1,0:T(8,128)(2,1)} fusion(bf16[128,16,128]{2,0,1:T(8,128)(2,1)S(1)} %get-tuple-element.188, s32[1024]{0:T(1024)S(1)} %pad_clamp_fusion.11), kind=kCustom, calls=%fused_computation.1.clone.clone.1 | custom fusion | bytes 4194560 | tf_op jit(solution)/shard_map/while/body/jit(_take)/gather | solution.py:41
  100.2 2.1 %gather_fusion.3 = bf16[64,128,128]{2,1,0:T(8,128)(2,1)} fusion(bf16[16,128,128]{2,1,0:T(8,128)(2,1)S(1)} %get-tuple-element.186, s32[1024]{0:T(1024)S(1)} %pad_clamp_fusion.12), kind=kCustom, calls=%fused_computation.clone.clone.1 | custom fusion | bytes 4194560 | tf_op jit(solution)/shard_map/while/body/jit(_take)/gather | solution.py:42
  102.3 0.6 compare_convert_fusion.2
  103.0 5.1 %fusion.64 = f32[128,128]{1,0:T(8,128)S(1)} fusion(f32[128,128]{1,0:T(8,128)S(1)} %get-tuple-element.171, bf16[64,128,128]{2,1,0:T(8,128)(2,1)} %multiply_convert_fusion.4, bf16[64,128,128]{2,1,0:T(8,128)(2,1)} %gather_fusion.2, bf16[64,128,128]{2,1,0:T(8,128)(2,1)} %gather_fusion.3, pred[64]{0:T(512)(128)(4,1)S(1)} %get-tuple-element.156, ...), kind=kOutput, calls=%fused_computation.20.clone.1 | convolution fusion | flops 542130176 | bytes 6422784 | tf_op jit(solution)/shard_map/while/body/gxa,gay->xy/dot_general | solution.py:55
  108.1 0.6 fusion.50
  108.7 100.1 %all-gather = bf16[2048,128]{1,0:T(8,128)(2,1)S(1)} all-gather(bf16[128,128]{1,0:T(8,128)(2,1)S(1)} %multiply_convert_fusion.2), channel_id=2, replica_groups=mesh['grp'=2,'had'=16] {'had'}, dimensions={0}, use_global_device_ids=true | all-gather | bytes 557056 | tf_op jit(solution)/shard_map/all_gather | solution.py:64
  208.8 0.4 fusion.35
  209.2 0.4 fusion.37
  209.6 0.9 fusion.34
  (28 shorter events, 0.2 us)
Async XLA Ops:
  0.6 1.4 copy-start
  2.1 11.0 %copy-start.2 = (s32[8,2]{0,1:T(2,128)S(1)}, s32[8,2]{0,1:T(2,128)}, u32[]{:S(2)}) copy-start(s32[8,2]{0,1:T(2,128)} %param.21) | copy-start | bytes 196
  2.1 24.6 %copy-start.1 = (bf16[16,128,128]{2,1,0:T(8,128)(2,1)S(1)}, bf16[16,128,128]{2,1,0:T(8,128)(2,1)}, u32[]{:S(2)}) copy-start(bf16[16,128,128]{2,1,0:T(8,128)(2,1)} %param.15) | copy-start | bytes 1572868
  5.0 21.7 %all-to-all-start = ((bf16[128,16,128]{2,0,1:T(8,128)(2,1)}), bf16[128,16,128]{2,0,1:T(8,128)(2,1)S(1)}, u32[]{:S(2)}, u32[]{:S(2)}) async-start(bf16[128,16,128]{2,0,1:T(8,128)(2,1)} %select_bitcast_fusion), calls=%async_computation | async-start | bytes 1048576 | tf_op jit(solution)/shard_map/all_to_all | solution.py:33
where the time goes:
time: 211 us
  blocking collectives  100 us (47%)
  matrix products  44.2 us (21%)
  local copies, waits for them, and re-layouts  37.9 us (18%)
  waiting for transfers between devices  13.6 us (6%)
  starting transfers between devices  7.41 us (4%)
  other arithmetic  5.68 us (3%)
    all_gather x1, blocking collectives, shards(): shard_rows = lax.all_gather(edge_local, 'had', axis=0, tiled=True)  100 us
    dot_general x4, matrix products, factor(): jnp.einsum('gxb,agb->gxa', resident, gathered, preferred_element_type=jnp...  20.8 us
    dot_general x4, matrix products, accumulate(): jnp.einsum('gxa,gay->xy', left_side, right_side, preferred_element_type=j...  20.3 us
    gather x8, local copies, waits for them, and re-layouts, factor(): resident = jnp.take(sink_slabs, sinks, axis=0)  17.1 us
    gather x8, local copies, waits for them, and re-layouts, factor(): gathered = jnp.take(received, slots, axis=1)  17.1 us
    all_to_all x1, waiting for transfers between devices, shards(): lax.all_to_all(outgoing, 'had', split_axis=1, concat_axis=1, tiled=True)  13.6 us
    all_to_all x1, starting transfers between devices, shards(): lax.all_to_all(outgoing, 'had', split_axis=1, concat_axis=1, tiled=True)  7.41 us
  transfers between devices with their start and end apart: 1, of which 1 were waited for; matrix products, arithmetic and copies ran while one was open for 0% of the time, Pallas kernels for 0%

commit v1 on v0

--- a/solution.py
+++ b/solution.py
@@ -30,7 +30,9 @@
         "xjb,yb->xjy", first_turn, local_peram[1], preferred_element_type=jnp.float32
     ).astype(jnp.bfloat16)
     outgoing = jnp.take(second_turn, pick_row, axis=1)
-    received = lax.all_to_all(outgoing, "had", split_axis=1, concat_axis=1, tiled=True)
+    parts = jnp.split(outgoing, lax.axis_size("had"), axis=1)
+    got = lax.all_to_all(jnp.stack(parts), "had", 0, 0)
+    received = jnp.concatenate(got, axis=1)
     graph_rows = graph_slot.shape[1]
     block_width = min(64, graph_rows)
     slot_table = graph_slot[0]

time: 211 us -> 220 us (1.043)
  local copies, waits for them, and re-layouts: 37.9 us -> 47.6 us
    unnamed x6 -> x21, local copies, waits for them, and re-layouts: 0.02 us -> 9.1 us
where the time goes in v1:
time: 220 us; the launch traced here: 219 us
  blocking collectives  100 us (45%)
  local copies, waits for them, and re-layouts  47.6 us (22%)
  matrix products  44.2 us (20%)
  waiting for transfers between devices  13.6 us (6%)
  starting transfers between devices  7.41 us (3%)
  other arithmetic  4.88 us (2%)
    all_gather x1, blocking collectives, shards(): shard_rows = lax.all_gather(edge_local, 'had', axis=0, tiled=True)  100 us
    dot_general x4, matrix products, factor(): jnp.einsum('gxb,agb->gxa', resident, gathered, preferred_element_type=jnp...  20.8 us
    dot_general x4, matrix products, accumulate(): jnp.einsum('gxa,gay->xy', left_side, right_side, preferred_element_type=j...  20.3 us
    gather x8, local copies, waits for them, and re-layouts, factor(): resident = jnp.take(sink_slabs, sinks, axis=0)  17.1 us
    gather x8, local copies, waits for them, and re-layouts, factor(): gathered = jnp.take(received, slots, axis=1)  17.1 us
    all_to_all x1, waiting for transfers between devices, shards(): got = lax.all_to_all(jnp.stack(parts), 'had', 0, 0)  13.6 us
    unnamed x21, local copies, waits for them, and re-layouts  9.1 us
    all_to_all x1, starting transfers between devices, shards(): got = lax.all_to_all(jnp.stack(parts), 'had', 0, 0)  7.41 us
  transfers between devices with their start and end apart: 1, of which 1 were waited for; matrix products, arithmetic and copies ran while one was open for 0% of the time, Pallas kernels for 0%

profile of v1, /device:TPU:0, one launch (start us, length us, event | category | flops | bytes accessed | tf_op | source)
XLA Modules:
  0.0 219.4 jit_solution(14772571454816507399)
XLA Ops:
  0.6 0.0 copy-start
  0.7 0.7 fusion.61
  1.4 0.7 compare_and_fusion.4
  2.1 1.3 convolution_convert_fusion
  3.3 0.0 copy-start.2
  3.3 0.0 copy-start.1
  3.3 0.6 gather_fusion.4
  4.0 0.1 select_bitcast_fusion
  4.1 0.6 fusion.54
  4.7 0.6 fusion.53
  5.3 0.6 fusion.52
  5.9 0.6 fusion.51
  6.5 0.6 fusion.50
  7.2 0.6 fusion.49
  7.8 0.6 fusion.48
  8.4 0.6 fusion.47
  9.0 0.6 fusion.46
  9.6 0.6 fusion.45
  10.2 0.6 fusion.44
  10.8 0.6 fusion.43
  11.4 0.6 fusion.42
  12.0 0.6 fusion.41
  12.6 0.6 fusion.40
  13.2 0.6 fusion.39
  13.8 7.4 %all-to-all-start = ((bf16[16,128,1,128]{3,1,2,0:T(8,128)(2,1)}), bf16[16,128,1,128]{3,1,2,0:T(8,128)(2,1)S(1)}, u32[]{:S(2)}, u32[]{:S(2)}) async-start(bf16[16,128,1,128]{3,1,2,0:T(8,128)(2,1)} %fusion.39), calls=%async_computation | async-start | bytes 1048576 | tf_op jit(solution)/shard_map/all_to_all | solution.py:34
  21.9 13.6 %all-to-all-done = bf16[16,128,1,128]{3,1,2,0:T(8,128)(2,1)S(1)} async-done(((bf16[16,128,1,128]{3,1,2,0:T(8,128)(2,1)}), bf16[16,128,1,128]{3,1,2,0:T(8,128)(2,1)S(1)}, u32[]{:S(2)}, u32[]{:S(2)}) %all-to-all-start) | async-done | bytes 524320 | tf_op jit(solution)/shard_map/all_to_all | solution.py:34
  35.5 81.4 %while.10 = (s32[]{:T(128)}, f32[128,128]{1,0:T(8,128)S(1)}, s32[]{:T(128)}, s32[512,2]{0,1:T(2,128)}, bf16[16,128,128]{2,1,0:T(8,128)(2,1)S(1)}, /*index=5*/s32...) while((s32[]{:T(128)}, f32[128,128]{1,0:T(8,128)S(1)}, ...), condition=%wide.region_1.4_spmd, body=%wide.region_0.3_spmd.sunk | while | flops 814765760 | bytes 29514672 | solution.py:62
  35.5 0.8 constant_dynamic-slice_fusion.3
  36.3 2.1 gather_fusion
  38.5 2.1 gather_fusion.1
  40.6 5.2 %multiply_convert_fusion.4 = bf16[64,128,128]{2,1,0:T(8,128)(2,1)} fusion(bf16[64,128,128]{2,1,0:T(8,128)(2,1)} %gather_fusion, bf16[64,128,128]{2,1,0:T(8,128)(2,1)} %gather_fusion.1, pred[64]{0:T(512)(128)(4,1)S(1)} %get-tuple-element.152, pred[64]{0:T(512)(128)(4,1)S(1)} %get-tuple-element.153), kind=kOutput, calls=%fused_computation.5.clone.1 | convolution fusion | flops 272629760 | bytes 6291584 | tf_op jit(solution)/shard_map/while/body/gxb,agb->gxa/dot_general | solution.py:45
  45.9 2.1 gather_fusion.2
  48.0 2.1 gather_fusion.3
  50.1 0.6 compare_convert_fusion.2
  50.8 5.1 %fusion.80 = f32[128,128]{1,0:T(8,128)S(1)} fusion(f32[128,128]{1,0:T(8,128)S(1)} %get-tuple-element.171, bf16[64,128,128]{2,1,0:T(8,128)(2,1)} %multiply_convert_fusion.4, bf16[64,128,128]{2,1,0:T(8,128)(2,1)} %gather_fusion.2, bf16[64,128,128]{2,1,0:T(8,128)(2,1)} %gather_fusion.3, pred[64]{0:T(512)(128)(4,1)S(1)} %get-tuple-element.156, ...), kind=kOutput, calls=%fused_computation.20.clone.1 | convolution fusion | flops 542130176 | bytes 6422784 | tf_op jit(solution)/shard_map/while/body/gxa,gay->xy/dot_general | solution.py:57
  55.9 0.8 constant_dynamic-slice_fusion.3
  56.7 2.1 gather_fusion
  58.9 2.1 gather_fusion.1
  61.0 5.2 %multiply_convert_fusion.4 = bf16[64,128,128]{2,1,0:T(8,128)(2,1)} fusion(bf16[64,128,128]{2,1,0:T(8,128)(2,1)} %gather_fusion, bf16[64,128,128]{2,1,0:T(8,128)(2,1)} %gather_fusion.1, pred[64]{0:T(512)(128)(4,1)S(1)} %get-tuple-element.152, pred[64]{0:T(512)(128)(4,1)S(1)} %get-tuple-element.153), kind=kOutput, calls=%fused_computation.5.clone.1 | convolution fusion | flops 272629760 | bytes 6291584 | tf_op jit(solution)/shard_map/while/body/gxb,agb->gxa/dot_general | solution.py:45
  66.2 2.1 gather_fusion.2
  68.3 2.1 gather_fusion.3
  70.5 0.6 compare_convert_fusion.2
  71.1 5.1 %fusion.80 = f32[128,128]{1,0:T(8,128)S(1)} fusion(f32[128,128]{1,0:T(8,128)S(1)} %get-tuple-element.171, bf16[64,128,128]{2,1,0:T(8,128)(2,1)} %multiply_convert_fusion.4, bf16[64,128,128]{2,1,0:T(8,128)(2,1)} %gather_fusion.2, bf16[64,128,128]{2,1,0:T(8,128)(2,1)} %gather_fusion.3, pred[64]{0:T(512)(128)(4,1)S(1)} %get-tuple-element.156, ...), kind=kOutput, calls=%fused_computation.20.clone.1 | convolution fusion | flops 542130176 | bytes 6422784 | tf_op jit(solution)/shard_map/while/body/gxa,gay->xy/dot_general | solution.py:57
  76.2 0.8 constant_dynamic-slice_fusion.3
  77.0 2.1 gather_fusion
  79.2 2.1 gather_fusion.1
  81.3 5.2 %multiply_convert_fusion.4 = bf16[64,128,128]{2,1,0:T(8,128)(2,1)} fusion(bf16[64,128,128]{2,1,0:T(8,128)(2,1)} %gather_fusion, bf16[64,128,128]{2,1,0:T(8,128)(2,1)} %gather_fusion.1, pred[64]{0:T(512)(128)(4,1)S(1)} %get-tuple-element.152, pred[64]{0:T(512)(128)(4,1)S(1)} %get-tuple-element.153), kind=kOutput, calls=%fused_computation.5.clone.1 | convolution fusion | flops 272629760 | bytes 6291584 | tf_op jit(solution)/shard_map/while/body/gxb,agb->gxa/dot_general | solution.py:45
  86.6 2.1 gather_fusion.2
  88.7 2.1 gather_fusion.3
  90.8 0.6 compare_convert_fusion.2
  91.5 5.1 %fusion.80 = f32[128,128]{1,0:T(8,128)S(1)} fusion(f32[128,128]{1,0:T(8,128)S(1)} %get-tuple-element.171, bf16[64,128,128]{2,1,0:T(8,128)(2,1)} %multiply_convert_fusion.4, bf16[64,128,128]{2,1,0:T(8,128)(2,1)} %gather_fusion.2, bf16[64,128,128]{2,1,0:T(8,128)(2,1)} %gather_fusion.3, pred[64]{0:T(512)(128)(4,1)S(1)} %get-tuple-element.156, ...), kind=kOutput, calls=%fused_computation.20.clone.1 | convolution fusion | flops 542130176 | bytes 6422784 | tf_op jit(solution)/shard_map/while/body/gxa,gay->xy/dot_general | solution.py:57
  96.6 0.8 constant_dynamic-slice_fusion.3
  97.4 2.1 gather_fusion
  99.6 2.1 gather_fusion.1
  101.7 5.2 %multiply_convert_fusion.4 = bf16[64,128,128]{2,1,0:T(8,128)(2,1)} fusion(bf16[64,128,128]{2,1,0:T(8,128)(2,1)} %gather_fusion, bf16[64,128,128]{2,1,0:T(8,128)(2,1)} %gather_fusion.1, pred[64]{0:T(512)(128)(4,1)S(1)} %get-tuple-element.152, pred[64]{0:T(512)(128)(4,1)S(1)} %get-tuple-element.153), kind=kOutput, calls=%fused_computation.5.clone.1 | convolution fusion | flops 272629760 | bytes 6291584 | tf_op jit(solution)/shard_map/while/body/gxb,agb->gxa/dot_general | solution.py:45
  106.9 2.1 gather_fusion.2
  109.0 2.1 gather_fusion.3
  111.2 0.6 compare_convert_fusion.2
  111.8 5.1 %fusion.80 = f32[128,128]{1,0:T(8,128)S(1)} fusion(f32[128,128]{1,0:T(8,128)S(1)} %get-tuple-element.171, bf16[64,128,128]{2,1,0:T(8,128)(2,1)} %multiply_convert_fusion.4, bf16[64,128,128]{2,1,0:T(8,128)(2,1)} %gather_fusion.2, bf16[64,128,128]{2,1,0:T(8,128)(2,1)} %gather_fusion.3, pred[64]{0:T(512)(128)(4,1)S(1)} %get-tuple-element.156, ...), kind=kOutput, calls=%fused_computation.20.clone.1 | convolution fusion | flops 542130176 | bytes 6422784 | tf_op jit(solution)/shard_map/while/body/gxa,gay->xy/dot_general | solution.py:57
  116.9 0.6 fusion.66
  117.6 100.1 %all-gather = bf16[2048,128]{1,0:T(8,128)(2,1)S(1)} all-gather(bf16[128,128]{1,0:T(8,128)(2,1)S(1)} %multiply_convert_fusion.2), channel_id=2, replica_groups=mesh['grp'=2,'had'=16] {'had'}, dimensions={0}, use_global_device_ids=true | all-gather | bytes 557056 | tf_op jit(solution)/shard_map/all_gather | solution.py:66
  217.7 0.4 fusion.35
  218.1 0.4 fusion.37
  218.5 0.9 fusion.34
  (31 shorter events, 0.2 us)
Async XLA Ops:
  0.6 1.4 copy-start
  3.3 18.6 %copy-start.2 = (s32[8,2]{0,1:T(2,128)S(1)}, s32[8,2]{0,1:T(2,128)}, u32[]{:S(2)}) copy-start(s32[8,2]{0,1:T(2,128)} %param.21) | copy-start | bytes 196
  3.3 32.2 %copy-start.1 = (bf16[16,128,128]{2,1,0:T(8,128)(2,1)S(1)}, bf16[16,128,128]{2,1,0:T(8,128)(2,1)}, u32[]{:S(2)}) copy-start(bf16[16,128,128]{2,1,0:T(8,128)(2,1)} %param.15) | copy-start | bytes 1572868
  13.8 21.7 %all-to-all-start = ((bf16[16,128,1,128]{3,1,2,0:T(8,128)(2,1)}), bf16[16,128,1,128]{3,1,2,0:T(8,128)(2,1)S(1)}, u32[]{:S(2)}, u32[]{:S(2)}) async-start(bf16[16,128,1,128]{3,1,2,0:T(8,128)(2,1)} %fusion.39), calls=%async_computation | async-start | bytes 1048576 | tf_op jit(solution)/shard_map/all_to_all | solution.py:34
